TPU v7x, 32 devices: a whole 2x2x4 slice. The times are simulated.
32 devices in a mesh: grp: 8 (over z, core), dev: 4 (over y, x).
Axes of the slice: x: 2, y: 2, z: 4, core: 2. Of those that a mesh axis runs over, the one named last changes fastest.
Arguments:
- tokens: bfloat16 [4096, 2304], P(('grp', 'dev')), may hold values from -6 to 6
- cotangent: bfloat16 [4096, 2304], P(('grp', 'dev')), may hold values from -6 to 6
- expert_ids: int32 [4096, 8], P(('grp', 'dev')), may hold values from 0 to 31, as said below
- combine_weights: bfloat16 [4096, 8], P(('grp', 'dev')), may hold values from 0.099609375 to 0.3984375
- live_counts: int32 [32, 2], P(('grp', 'dev')), may hold values from 32 to 64, as said below
- gate_weight: bfloat16 [32, 2304, 512], P(('grp', 'dev')), may hold values from -0.125 to 0.125
- up_weight: bfloat16 [32, 2304, 512], P(('grp', 'dev')), may hold values from -0.125 to 0.125
- down_weight: bfloat16 [32, 512, 2304], P(('grp', 'dev')), may hold values from -0.25 to 0.25
Outputs:
- mixed_out: bfloat16 [4096, 2304], P(('grp', 'dev'))
- input_grad: bfloat16 [4096, 2304], P(('grp', 'dev'))
Inputs may be any that keep to these rules, and one draw needn't show every extreme that they name: `expert_ids`: expert g * 4 + l is expert l of group g. Each row names 8 distinct experts lying in 4 distinct groups, 2 in each, and entries 2 q to 2 q + 1 share one group. Counting all 64 rows of one device's micro-batch, live or not, each expert is named by exactly 16 rows and each group by exactly 32 rows; so at most 16 live rows name one expert, exactly 16 in a full micro-batch. The first live_counts[d, m] rows of device d's micro-batch m are live, the others are padding; some micro-batch of some device is full.
All inputs are finite; a program needn't handle non-finite values.
Results may differ from a plain program's by a relative error of at most 0.0085.
Values may be sent and summed in bfloat16 or wider, within the bound.
A program may use at most 128 MiB of HBM per device.

v0:
```python
import functools

import jax
import jax.numpy as jnp
from jax import lax
from jax.experimental import pallas as pl
from jax.experimental.pallas import tpu as pltpu
from jax.sharding import PartitionSpec as P

PAIR = 2
LAG_EXPERT = 1
LAG_RETURN = 2
MESH = pl.DeviceIdType.MESH
TRANS_RHS = (((1,), (1,)), ((), ()))


def xor(a, b, size):
    out = 0
    bit = 1
    while bit < size:
        out = out + ((a // bit + b // bit) % 2) * bit
        bit *= 2
    return out


def chunk_order(groups):
    if groups < 8:
        return list(range(groups))
    return [0, 4, 2] + list(range(5, groups)) + [3, 1]


def distance_of(unit, parts, groups):
    i = unit // parts
    out = 0
    for k, value in enumerate(chunk_order(groups)):
        out = out + value * ((i + groups - k) // groups - (i + groups - k - 1) // groups)
    return out


def moe_kernel(
    groups,
    peers,
    joined,
    parts,
    tok_ref,
    cot_ref,
    pick_ref,
    slot_ref,
    sum_ref,
    gate_hbm,
    up_hbm,
    down_hbm,
    out_ref,
    grad_ref,
    gate_ref,
    up_ref,
    down_ref,
    zsend,
    zrecv,
    zback,
    xysend,
    xyrecv,
    xyback,
    w_sem,
    zs_sem,
    zr_sem,
    bs_sem,
    br_sem,
    ds_sem,
    dr_sem,
    rs_sem,
    rr_sem,
):
    g = lax.axis_index("grp")
    l = lax.axis_index("dev")
    width = tok_ref.shape[1]
    wide = 2 * width
    units = groups * parts
    chunks = units // joined
    group_rows = zrecv.shape[1]
    slots = slot_ref.shape[2]
    peer_rows = slots // peers

    barrier = pltpu.get_barrier_semaphore()
    for k in range(1, groups):
        pl.semaphore_signal(
            barrier, inc=1, device_id={"grp": xor(g, k, groups)}, device_id_type=MESH
        )
    for q in range(1, peers):
        pl.semaphore_signal(
            barrier, inc=1, device_id={"dev": xor(l, q, peers)}, device_id_type=MESH
        )

    loads = [
        pltpu.make_async_copy(src, dst, w_sem.at[n])
        for n, (src, dst) in enumerate(
            ((gate_hbm, gate_ref), (up_hbm, up_ref), (down_hbm, down_ref))
        )
    ]
    for load in loads:
        load.start()

    def z_copy(i):
        return pltpu.make_async_remote_copy(
            src_ref=zsend.at[i],
            dst_ref=zrecv.at[i],
            send_sem=zs_sem.at[i],
            recv_sem=zr_sem.at[i],
            device_id={"grp": xor(g, distance_of(i, parts, groups), groups)},
            device_id_type=MESH,
        )

    def z_back(i):
        return pltpu.make_async_remote_copy(
            src_ref=zrecv.at[i, :, pl.ds(0, wide)],
            dst_ref=zback.at[i],
            send_sem=bs_sem.at[i],
            recv_sem=br_sem.at[i],
            device_id={"grp": xor(g, distance_of(i, parts, groups), groups)},
            device_id_type=MESH,
        )

    def xy_copy(c, q):
        return pltpu.make_async_remote_copy(
            src_ref=xysend.at[c, q],
            dst_ref=xyrecv.at[c, q],
            send_sem=ds_sem.at[c, q],
            recv_sem=dr_sem.at[c, q],
            device_id={"dev": xor(l, q, peers)},
            device_id_type=MESH,
        )

    def xy_back(c, q):
        return pltpu.make_async_remote_copy(
            src_ref=xyrecv.at[c, q],
            dst_ref=xyback.at[c, q],
            send_sem=rs_sem.at[c, q],
            recv_sem=rr_sem.at[c, q],
            device_id={"dev": xor(l, q, peers)},
            device_id_type=MESH,
        )

    def fill(i, target):
        pick = pick_ref[i]
        for source, low in ((tok_ref, 0), (cot_ref, width)):
            target[i, :, low : low + width] = jnp.dot(
                pick, source[...], preferred_element_type=jnp.float32
            ).astype(jnp.bfloat16)
        target[i, :, wide : wide + slots] = jnp.dot(
            pick, slot_ref[i // parts], preferred_element_type=jnp.float32
        ).astype(jnp.bfloat16)

    for i in range(parts):
        fill(i, zrecv)

    def chunk_weights(c):
        block = zrecv[pl.ds(c * joined, joined), :, wide : wide + slots]
        return block.reshape(joined * group_rows, slots)

    def place(c):
        for j in range(joined):
            i = c * joined + j

            @pl.when(i >= parts)
            def _(i=i):
                z_copy(i).wait_recv()

        weights = chunk_weights(c).astype(jnp.float32)
        select = jnp.where(weights != 0.0, 1.0, 0.0).T.astype(jnp.bfloat16)
        rows = zrecv[pl.ds(c * joined, joined), :, 0:wide].reshape(joined * group_rows, wide)
        placed = jnp.dot(select, rows, preferred_element_type=jnp.float32).astype(jnp.bfloat16)
        for q in range(1, peers):
            xysend[c, q] = placed[q * peer_rows : (q + 1) * peer_rows]
            xy_copy(c, q).start()
        xyrecv[c, 0] = placed[0:peer_rows]

    def expert(c):
        @pl.when(c == 0)
        def _():
            for load in loads:
                load.wait()

        for q in range(1, peers):
            xy_copy(c, q).wait_recv()
        rows_x = xyrecv[c, :, :, 0:width].reshape(slots, width)
        rows_dy = xyrecv[c, :, :, width:wide].reshape(slots, width)
        gate_pre = jnp.dot(rows_x, gate_ref[...], preferred_element_type=jnp.float32)
        up_pre = jnp.dot(rows_x, up_ref[...], preferred_element_type=jnp.float32)
        act_grad = lax.dot_general(
            rows_dy, down_ref[...], TRANS_RHS, preferred_element_type=jnp.float32
        )
        sig = jax.nn.sigmoid(gate_pre)
        gate_act = gate_pre * sig
        act = (gate_act * up_pre).astype(jnp.bfloat16)
        gate_grad = (act_grad * up_pre * sig * (1.0 + gate_pre * (1.0 - sig))).astype(jnp.bfloat16)
        up_grad = (act_grad * gate_act).astype(jnp.bfloat16)
        expert_out = jnp.dot(act, down_ref[...], preferred_element_type=jnp.float32)
        xyrecv[c, :, :, 0:width] = expert_out.astype(jnp.bfloat16).reshape(peers, peer_rows, width)
        expert_grad = lax.dot_general(
            gate_grad, gate_ref[...], TRANS_RHS, preferred_element_type=jnp.float32
        ) + lax.dot_general(up_grad, up_ref[...], TRANS_RHS, preferred_element_type=jnp.float32)
        xyrecv[c, :, :, width:wide] = expert_grad.astype(jnp.bfloat16).reshape(
            peers, peer_rows, width
        )
        for q in range(1, peers):
            xy_back(c, q).start()
        xyback[c, 0] = xyrecv[c, 0]

    def combine(c):
        for q in range(1, peers):
            xy_back(c, q).wait_recv()
        weights = chunk_weights(c)
        pairs = jnp.dot(
            weights, xyback[c].reshape(slots, wide), preferred_element_type=jnp.float32
        ).astype(jnp.bfloat16)
        zrecv[pl.ds(c * joined, joined), :, 0:wide] = pairs.reshape(joined, group_rows, wide)
        for j in range(joined):
            i = c * joined + j

            @pl.when(i >= parts)
            def _():
                z_back(i).start()

    early = min(1, parts // joined)
    pl.semaphore_wait(barrier, groups + peers - 2)
    for c in range(early):
        place(c)
    fill(parts, zsend)

    def send_step(i, carry):
        fill(i, zsend)
        z_copy(i - 1).start()
        return carry

    lax.fori_loop(parts + 1, units, send_step, 0)
    z_copy(units - 1).start()

    def step(t, carry):
        @pl.when((t >= early) & (t < chunks))
        def _():
            place(t)

        @pl.when((t >= LAG_EXPERT) & (t < chunks + LAG_EXPERT))
        def _():
            expert(t - LAG_EXPERT)

        @pl.when(t >= LAG_RETURN)
        def _():
            combine(t - LAG_RETURN)

        return carry

    lax.fori_loop(0, chunks + LAG_RETURN, step, 0)

    for i in range(parts):
        zback[i] = zrecv[i, :, 0:wide]

    def finish_step(i, carry):
        z_back(i).wait_recv()
        return carry

    lax.fori_loop(parts, units, finish_step, 0)
    for target, low in ((out_ref, 0), (grad_ref, width)):
        target[...] = jnp.dot(
            sum_ref[...],
            zback[:, :, low : low + width].reshape(units * group_rows, width),
            preferred_element_type=jnp.float32,
        ).astype(jnp.bfloat16)

    def drain_z(i, carry):
        z_copy(i).wait_send()
        z_back(i).wait_send()
        return carry

    lax.fori_loop(parts, units, drain_z, 0)

    def drain_xy(c, carry):
        for q in range(1, peers):
            xy_copy(c, q).wait_send()
            xy_back(c, q).wait_send()
        return carry

    lax.fori_loop(0, chunks, drain_xy, 0)


def routing(expert_ids, combine_weights, live_counts, groups, peers, joined):
    rows, top_count = expert_ids.shape
    parts = live_counts.shape[1]
    rows_mb = rows // parts
    experts = groups * peers
    units = groups * parts
    per_expert = rows_mb * top_count // experts
    per_group = per_expert * peers // PAIR
    g = lax.axis_index("grp")
    l = lax.axis_index("dev")
    relative = ((expert_ids // peers) ^ g) * peers + ((expert_ids % peers) ^ l)
    order = jnp.array(chunk_order(groups), jnp.int32)
    wanted = (order[:, None] * peers + jnp.arange(peers, dtype=jnp.int32)).reshape(-1)
    hit = relative[:, :, None] == wanted
    member = jnp.any(hit, axis=1)
    weight = jnp.sum(
        jnp.where(hit, combine_weights.astype(jnp.float32)[:, :, None], 0.0), axis=1
    )
    index = jnp.arange(rows, dtype=jnp.int32)
    part = index // rows_mb
    live = (index % rows_mb) < jnp.repeat(live_counts[0], rows_mb)
    weight = jnp.where(live[:, None], weight, 0.0).astype(jnp.bfloat16)
    in_group = jnp.any(member.reshape(rows, groups, peers), axis=2)
    both = jnp.concatenate([member, in_group], axis=1).astype(jnp.bfloat16)
    before = (
        (index[:, None] > index[None, :]) & (part[:, None] == part[None, :])
    ).astype(jnp.bfloat16)
    rank = jnp.dot(before, both, preferred_element_type=jnp.float32).astype(jnp.int32)
    expert_rank, group_rank = rank[:, :experts], rank[:, experts:]
    group_slot = jnp.where(in_group, group_rank + part[:, None] * per_group, -1)
    unit_rows = jnp.arange(parts * per_group, dtype=jnp.int32)
    pick = (
        (group_slot.T[:, None, :] == unit_rows[None, :, None])
        .astype(jnp.bfloat16)
        .reshape(units, per_group, rows)
    )
    total = (
        (group_slot[:, :, None] == unit_rows)
        .astype(jnp.bfloat16)
        .reshape(rows, units * per_group)
    )
    width = joined * per_expert
    offset = jnp.arange(groups, dtype=jnp.int32)[None, :] * parts + part[:, None]
    expert_slot = expert_rank.reshape(rows, groups, peers) + (
        offset % joined * per_expert
    )[..., None]
    expert_slot = expert_slot.transpose(1, 0, 2)[..., None]
    slot = jnp.where(
        expert_slot == jnp.arange(width, dtype=jnp.int32),
        weight.reshape(rows, groups, peers).transpose(1, 0, 2)[..., None],
        jnp.zeros((), jnp.bfloat16),
    ).reshape(groups, rows, peers * width)
    return pick, slot, total


def local(
    tokens, cotangent, expert_ids, combine_weights, live_counts, gate_weight, up_weight, down_weight
):
    groups = lax.axis_size("grp")
    peers = lax.axis_size("dev")
    rows, width = tokens.shape
    hidden = gate_weight.shape[2]
    parts = live_counts.shape[1]
    units = groups * parts
    per_expert = rows // parts * expert_ids.shape[1] // (groups * peers)
    per_group = per_expert * peers // PAIR
    joined = max(1, 16 // per_expert)
    chunks = units // joined
    peer_rows = joined * per_expert
    slots = peers * peer_rows
    wide = 2 * width
    pick, slot, total = routing(
        expert_ids, combine_weights, live_counts, groups, peers, joined
    )
    vmem = pl.BlockSpec(memory_space=pltpu.VMEM)
    anywhere = pl.BlockSpec(memory_space=pl.ANY)
    dma = pltpu.SemaphoreType.DMA
    bf16 = jnp.bfloat16
    return pl.pallas_call(
        functools.partial(moe_kernel, groups, peers, joined, parts),
        out_shape=(
            jax.ShapeDtypeStruct((rows, width), bf16),
            jax.ShapeDtypeStruct((rows, width), bf16),
        ),
        in_specs=[vmem] * 5 + [anywhere] * 3,
        out_specs=(vmem, vmem),
        scratch_shapes=[
            pltpu.VMEM((width, hidden), bf16),
            pltpu.VMEM((width, hidden), bf16),
            pltpu.VMEM((hidden, width), bf16),
            pltpu.VMEM((units, per_group, wide + slots), bf16),
            pltpu.VMEM((units, per_group, wide + slots), bf16),
            pltpu.VMEM((units, per_group, wide), bf16),
            pltpu.VMEM((chunks, peers, peer_rows, wide), bf16),
            pltpu.VMEM((chunks, peers, peer_rows, wide), bf16),
            pltpu.VMEM((chunks, peers, peer_rows, wide), bf16),
            dma((3,)),
            dma((units,)),
            dma((units,)),
            dma((units,)),
            dma((units,)),
            dma((chunks, peers)),
            dma((chunks, peers)),
            dma((chunks, peers)),
            dma((chunks, peers)),
        ],
        compiler_params=pltpu.CompilerParams(
            collective_id=0, has_side_effects=True, vmem_limit_bytes=65 * 1024 * 1000
        ),
    )(
        tokens,
        cotangent,
        pick,
        slot,
        total,
        gate_weight[0],
        up_weight[0],
        down_weight[0],
    )


def solution(mesh):
    spec2 = P(("grp", "dev"), None)
    spec3 = P(("grp", "dev"), None, None)
    return jax.shard_map(
        local,
        mesh=mesh,
        in_specs=(spec2,) * 5 + (spec3,) * 3,
        out_specs=(spec2, spec2),
        check_vma=False,
    )
```

profile of v0, /device:TPU:0, one launch (start us, length us, event | category | flops | bytes accessed | tf_op | source)
XLA Modules:
  0.0 234.7 jit_solution(11379799778235385655)
XLA Ops:
  0.7 0.7 broadcast_in_dim.38
  1.4 0.1 reshape.115
  1.5 0.1 eq.118
  1.6 0.7 fusion.12
  2.3 0.7 convert_element_type.22
  3.0 0.7 iota_add_fusion
  3.7 0.1 add.82
  3.8 0.1 compare_reduce_fusion
  3.9 0.1 fusion
  4.0 0.1 eq.124
  4.1 0.2 convolution_convert_fusion
  4.3 0.8 compare_convert_fusion.1.pick_ref
  5.2 0.2 copy.22
  5.4 0.2 copy.21
  5.6 0.8 compare_select_fusion.slot_ref
  6.4 0.1 copy.23
  6.5 0.7 compare_convert_fusion.sum_ref
  7.2 223.7 %shard_map.104 = (bf16[128,2304]{1,0:T(8,128)(2,1)}, bf16[128,2304]{1,0:T(8,128)(2,1)}) custom-call(bf16[128,2304]{1,0:T(8,128)(2,1)} %tok_ref.1, bf16[128,2304]{1,0:T(8,128)(2,1)} %cot_ref.1, bf16[16,32,128]{2,1,0:T(8,128)(2,1)} %compare_convert_fusion.1.pick_ref, bf16[8,128,64]{2,1,0:T(8,128)(2,1)} %compare_select_fusion.slot_ref, ...), custom_call_target="tpu_custom_call" | custom-call | tf_op jit(solution)/shard_map/pallas_call | solution.py:364
  230.9 1.9 copy.26
  232.8 1.9 copy.27
  (15 shorter events, 0.2 us)
where the time goes:
time: 235 us
  Pallas kernels  224 us (95%)
  local copies, waits for them, and re-layouts  5.46 us (2%)
  other arithmetic  4.6 us (2%)
    pallas_call x1, Pallas kernels, local(): pl.pallas_call(functools.partial(moe_kernel, groups, peers, joined, parts...  224 us

commit v1 on v0

--- a/solution.py
+++ b/solution.py
@@ -338,7 +338,7 @@
     return pick, slot, total
 
 
-def local(
+def general_local(
     tokens, cotangent, expert_ids, combine_weights, live_counts, gate_weight, up_weight, down_weight
 ):
     groups = lax.axis_size("grp")
@@ -404,6 +404,661 @@
     )
 
 
+LANES = 128
+
+
+PIECES = ((0, 0), (1, 0), (1, 1))
+ARRIVE, SELECT, EXPERT, COMBINE, PAIR_SUM, REDUCE = 0, 3, 5, 6, 8, 10
+OWN, PASS_OWN, FINAL, FINISH, IDLE = 13, 16, 17, 18, 19
+KINDS = 32
+PACKED = 3
+PLAN_PARTS = 2
+PLAN_4 = (
+    (
+        113, 129, 105, 120, 121, 2, 32, 24, 10, 18, 26, 34, 4, 40, 20, 42, 12, 28, 36, 50, 58,
+        6, 7, 44, 22, 14, 38, 30, 60, 15, 52, 23, 39, 31, 46, 68, 74, 3, 76, 47, 66, 62, 5, 54,
+        63, 19, 11, 55, 35, 27, 70, 71, 79, 21, 78, 13, 29, 37, 43, 45, 33, 51, 25, 61, 56, 53,
+        41, 77, 69, 48, 59, 136, 57, 49, 64, 67, 75, 137, 73, 72, 144, 65, 145,
+    ),
+    (
+        122, 131, 34, 26, 4, 1, 20, 12, 0, 28, 36, 7, 16, 6, 8, 22, 24, 32, 9, 17, 44, 14, 15,
+        30, 38, 52, 33, 23, 31, 39, 107, 46, 25, 68, 5, 123, 40, 115, 60, 21, 47, 54, 13, 29,
+        62, 100, 76, 37, 48, 84, 41, 63, 94, 56, 78, 27, 102, 55, 95, 35, 45, 88, 103, 57, 71,
+        79, 70, 92, 49, 64, 42, 89, 96, 97, 86, 43, 72, 73, 87, 61, 53, 65, 58, 80, 93, 59, 50,
+        101, 138, 51, 81, 77, 69, 85, 139, 66, 74, 67, 75, 146, 147,
+    ),
+)
+PLANS = {4: PLAN_4}
+
+
+def plan_words(depth, parts):
+    count = depth * parts
+    base = KINDS * count
+    orders = []
+    for z in range(depth):
+        codes = list(PLANS[depth][min(z, depth - 1 - z)])
+        if 2 * z >= depth:
+            codes = [
+                kind - kind % count + (depth - 1 - kind % count // parts) * parts + kind % parts
+                for kind in codes
+            ]
+        orders.append(codes)
+    length = max(len(codes) for codes in orders)
+    length += -length % PACKED
+    words = []
+    for codes in orders:
+        codes = codes + [IDLE * count] * (length - len(codes))
+        words.append(
+            [
+                sum(codes[b + n] * base**n for n in range(PACKED))
+                for b in range(0, length, PACKED)
+            ]
+        )
+    return words
+
+
+def plane_kernel(
+    groups,
+    parts,
+    experts,
+    per,
+    cut,
+    tok_hbm,
+    cot_hbm,
+    ids_ref,
+    mix_ref,
+    live_ref,
+    gate_hbm,
+    up_hbm,
+    down_hbm,
+    out_ref,
+    grad_ref,
+    gate_ref,
+    up_ref,
+    down_ref,
+    dense_a,
+    dense_b,
+    hot_ref,
+    slot_ref,
+    weight_ref,
+    send_ref,
+    moved_x,
+    moved_dy,
+    back_ref,
+    land_a,
+    land_b,
+    sum_a,
+    sum_b,
+    w_sem,
+    in_sem,
+    agr_sem,
+    agz_sem,
+    agd_sem,
+    agp_sem,
+    ss_sem,
+    sr_sem,
+    bs_sem,
+    br_sem,
+    ps_sem,
+    pr_sem,
+    ra_sem,
+    rb_sem,
+    rs_sem,
+    fs_sem,
+    fr_sem,
+):
+    g = lax.axis_index("grp")
+    l = lax.axis_index("dev")
+    depth = groups // 2
+    z = g // 2
+    core = g % 2
+    peers = experts // groups
+    rows_mb = dense_a.shape[4]
+    rows = rows_mb * parts
+    width = down_ref.shape[1]
+    rest = width - cut
+    count = depth * parts
+    pair = 2 * per
+    blocks = rows_mb // per
+    slots = 4 * pair
+    both = 2 * rows_mb
+    f32 = jnp.float32
+    bf16 = jnp.bfloat16
+    inner = (z > 0) & (z < depth - 1)
+    outer = (z == 0) | (z == depth - 1)
+    dense = (dense_a, dense_b)
+    size = (cut, rest)
+    outs = (out_ref, grad_ref)
+
+    flips = (l + 2 - 4 * (l // 2), l + 1 - 2 * (l % 2))
+
+    def near(h):
+        return {"grp": g, "dev": flips[1 - h]}
+
+    def peer(h, q):
+        return {
+            "grp": g + (q // 2) * (1 - 2 * core),
+            "dev": flips[h] if q % 2 else l,
+        }
+
+    def remote(src, dst, send, recv, device):
+        return pltpu.make_async_remote_copy(
+            src_ref=src,
+            dst_ref=dst,
+            send_sem=send,
+            recv_sem=recv,
+            device_id=device,
+            device_id_type=MESH,
+        )
+
+    def spread_z(h, k, p, s, m, d, second=False):
+        slot = dense[k].at[h, p, s, m]
+        send = agd_sem.at[2 * h + k, p, m] if second else agz_sem.at[2 * h + k, p, s, m]
+        return remote(
+            slot, slot, send, agr_sem.at[2 * h + k, p, s, m], {"grp": g + 2 * d, "dev": l}
+        )
+
+    def spread_p(h, k, s, m):
+        return remote(
+            dense[k].at[h, 0, s, m],
+            dense[k].at[h, 1, s, m],
+            agp_sem.at[2 * h + k, s, m],
+            agr_sem.at[2 * h + k, 1, s, m],
+            near(h),
+        )
+
+    def moved(h, t, q):
+        if h == 0:
+            return moved_x.at[t, q // 2, q % 2]
+        return moved_dy.at[t, q // 2, :, q % 2]
+
+    def select_copy(h, t, q):
+        return remote(
+            send_ref.at[h, t, pl.ds(2 * q, 2)],
+            moved(h, t, q),
+            ss_sem.at[h, t, q],
+            sr_sem.at[h, t, q],
+            peer(h, q),
+        )
+
+    def back_copy(h, t, q):
+        return remote(
+            moved(h, t, q),
+            back_ref.at[h, t, q],
+            bs_sem.at[h, t, q],
+            br_sem.at[h, t, q],
+            peer(h, q),
+        )
+
+    def sums(h, k, p, t):
+        low = 0 if k == 0 else cut
+        return send_ref.at[h, t, pl.ds(p * blocks, blocks), :, pl.ds(low, size[k])]
+
+    def pair_copy(h, t):
+        return remote(
+            sums(h, 0, 1, t), land_a.at[h, t], ps_sem.at[h, t], pr_sem.at[h, t], near(h)
+        )
+
+    def away(s):
+        return jnp.where(s > z, 1, -1)
+
+    def onward(h, k, p, s, m, src):
+        slot = jnp.where(s == z + 1, depth, s)
+        if k == 0:
+            dst, recv = sum_a.at[h, slot, m], ra_sem.at[h, slot, m]
+        else:
+            dst, recv = sum_b.at[h, p, slot, m], rb_sem.at[h, p, slot, m]
+        return remote(
+            src, dst, rs_sem.at[h, k + p, s, m], recv, {"grp": g + 2 * away(s), "dev": l}
+        )
+
+    def final_copy(h, m):
+        return remote(
+            sums(h, 1, 1, z * parts + m),
+            land_b.at[h, m],
+            fs_sem.at[h, m],
+            fr_sem.at[h, m],
+            near(h),
+        )
+
+    barrier = pltpu.get_barrier_semaphore()
+
+    def greet(device):
+        pl.semaphore_signal(barrier, inc=1, device_id=device, device_id_type=MESH)
+
+    @pl.when(z > 0)
+    def _():
+        greet({"grp": g - 2, "dev": l})
+
+    @pl.when(z < depth - 1)
+    def _():
+        greet({"grp": g + 2, "dev": l})
+
+    greet(peer(0, 2))
+    for h in range(2):
+        greet(peer(h, 1))
+        greet(peer(h, 3))
+
+    ins = []
+    for h, src in ((0, tok_hbm), (1, cot_hbm)):
+        for m in range(parts):
+            for k, low in ((1, cut), (0, 0)):
+                copy = pltpu.make_async_copy(
+                    src.at[pl.ds(m * rows_mb, rows_mb), pl.ds(low, size[k])],
+                    dense[k].at[h, 0, z, m, :, pl.ds(0, size[k])],
+                    in_sem.at[2 * h + k, m],
+                )
+                copy.start()
+                ins.append(copy)
+    loads = [
+        pltpu.make_async_copy(src, dst, w_sem.at[n])
+        for n, (src, dst) in enumerate(
+            ((gate_hbm, gate_ref), (up_hbm, up_ref), (down_hbm, down_ref))
+        )
+    ]
+    for load in loads:
+        load.start()
+
+    row = lax.broadcasted_iota(jnp.int32, (rows, LANES), 0)
+    lane = lax.broadcasted_iota(jnp.int32, (rows, LANES), 1)
+    ids = ids_ref[...]
+    mix = mix_ref[...].astype(f32)
+    weight = jnp.zeros((rows, LANES), f32)
+    named = jnp.zeros((rows, LANES), f32)
+    for k in range(ids.shape[1]):
+        expert_id = ids[:, k : k + 1]
+        weight = weight + jnp.where(lane == expert_id, mix[:, k : k + 1], 0.0)
+        named = named + jnp.where(lane == expert_id + experts, 1.0, 0.0)
+    lives = live_ref[...]
+    alive = jnp.zeros((rows, LANES), f32)
+    for m in range(parts):
+        first = m * rows_mb
+        alive = alive + jnp.where(
+            (row >= first) & (row < first + lives[0:1, m : m + 1]), 1.0, 0.0
+        )
+    row_a = lax.broadcasted_iota(jnp.int32, (rows, rows), 0)
+    row_b = lax.broadcasted_iota(jnp.int32, (rows, rows), 1)
+    before = jnp.where(
+        (row_a > row_b) & (lax.div(row_a, rows_mb) == lax.div(row_b, rows_mb)), 1.0, 0.0
+    ).astype(bf16)
+    rank = jnp.dot(before, named.astype(bf16), preferred_element_type=f32)
+    routes = jnp.where(lane < experts, weight * alive, rank).astype(bf16)
+    for h in range(2):
+        for m in range(parts):
+            dense_a[h, 0, z, m, :, cut : cut + LANES] = routes[m * rows_mb : (m + 1) * rows_mb]
+
+    lane_k = lax.broadcasted_iota(jnp.int32, (LANES, slots), 0)
+    slot_k = lax.broadcasted_iota(jnp.int32, (LANES, slots), 1)
+    quad = lax.div(slot_k, pair)
+    owner = 2 * z + core + lax.div(quad, 2) * (1 - 2 * core)
+    for h in range(2):
+        target = owner * peers + jnp.where(lax.rem(quad, 2) == 1, flips[h], l)
+        hot_ref[h, 0] = jnp.where(lane_k == target, 1.0, 0.0).astype(bf16)
+        hot_ref[h, 1] = jnp.where(lane_k == target + experts, 1.0, 0.0).astype(bf16)
+    row_s = lax.broadcasted_iota(jnp.int32, (both, slots), 0)
+    col_s = lax.broadcasted_iota(jnp.int32, (both, slots), 1)
+    slot_ref[...] = jnp.where(
+        lax.div(row_s, rows_mb) == lax.rem(lax.div(col_s, per), 2), lax.rem(col_s, per), -1
+    ).astype(f32)
+
+    for copy in ins:
+        copy.wait()
+    pl.semaphore_wait(barrier, 5 + jnp.where(inner, 2, 1))
+
+    def send_own(h, k, p, m):
+        @pl.when(z < depth - 1)
+        def _():
+            spread_z(h, k, p, z, m, 1).start()
+
+        @pl.when(z > 0)
+        def _():
+            spread_z(h, k, p, z, m, -1, True).start()
+
+    def spread_own(k, p, m):
+        for h in range(2):
+            if p == 1:
+                spread_p(h, 1, z, m).wait_recv()
+            send_own(h, k, p, m)
+
+    def pass_own(k, m):
+        for h in range(2):
+            spread_p(h, k, z, m).start()
+
+    pass_own(1, 0)
+    spread_own(0, 0, 0)
+    spread_own(1, 0, 0)
+    pass_own(0, 0)
+    for m in range(1, parts):
+        pass_own(1, m)
+    for load in loads:
+        load.wait()
+
+    def arrive(k, p, s, m):
+        for h in range(2):
+            copy = spread_z(h, k, p, s, m, -away(s))
+            copy.wait_recv()
+            if k == 0:
+                spread_p(h, 0, s, m).start()
+
+            @pl.when(inner)
+            def _(copy=copy):
+                copy.start()
+
+    def select(h, t, s, m):
+        spread_p(h, 0, s, m).wait_recv()
+        routes = dense_a[h, :, s, m, :, cut : cut + LANES].reshape(both, LANES)
+        weights = jnp.dot(routes, hot_ref[h, 0], preferred_element_type=f32)
+        ranks = jnp.dot(routes, hot_ref[h, 1], preferred_element_type=f32)
+        weights = jnp.where(ranks == slot_ref[...], weights, 0.0)
+        weight_ref[h, t] = weights.astype(bf16)
+        pick = jnp.where(weights != 0.0, 1.0, 0.0).T.astype(bf16)
+        for k, low in ((0, 0), (1, cut)):
+            span = slice(low, low + size[k])
+            placed = jnp.dot(
+                pick,
+                dense[k][h, :, s, m, :, 0 : size[k]].reshape(both, size[k]),
+                preferred_element_type=f32,
+            ).astype(bf16)
+            kept = placed[0:pair].reshape(2, per, size[k])
+            if h == 0:
+                moved_x[t, 0, 0, :, :, span] = kept
+            else:
+                moved_dy[t, 0, :, 0, :, span] = kept
+            send_ref[h, t, 2:8, :, span] = placed[pair:slots].reshape(6, per, size[k])
+        for q in range(1, 4):
+            select_copy(h, t, q).start()
+
+    def expert(t):
+        for h in range(2):
+            for q in range(1, 4):
+                select_copy(h, t, q).wait_recv()
+        rows_x = moved_x[t].reshape(slots, width)
+        rows_dy = moved_dy[t].reshape(slots, width)
+        gate_pre = jnp.dot(rows_x, gate_ref[...], preferred_element_type=f32)
+        up_pre = jnp.dot(rows_x, up_ref[...], preferred_element_type=f32)
+        act_grad = lax.dot_general(
+            rows_dy, down_ref[...], TRANS_RHS, preferred_element_type=f32
+        )
+        sig = jax.nn.sigmoid(gate_pre)
+        gate_act = gate_pre * sig
+        act = (gate_act * up_pre).astype(bf16)
+        gate_grad = (act_grad * up_pre * sig * (1.0 + gate_pre * (1.0 - sig))).astype(bf16)
+        up_grad = (act_grad * gate_act).astype(bf16)
+        expert_out = jnp.dot(act, down_ref[...], preferred_element_type=f32)
+        moved_x[t] = expert_out.astype(bf16).reshape(2, 2, 2, per, width)
+        for q in range(1, 4):
+            back_copy(0, t, q).start()
+        expert_grad = lax.dot_general(
+            gate_grad, gate_ref[...], TRANS_RHS, preferred_element_type=f32
+        ) + lax.dot_general(up_grad, up_ref[...], TRANS_RHS, preferred_element_type=f32)
+        moved_dy[t] = expert_grad.astype(bf16).reshape(2, 2, 2, per, width)
+        for q in range(1, 4):
+            back_copy(1, t, q).start()
+        back_ref[0, t, 0] = moved_x[t, 0, 0]
+        back_ref[1, t, 0] = moved_dy[t, 0, :, 0]
+
+    def combine(h, t, s, m):
+        for q in range(1, 4):
+            back_copy(h, t, q).wait_recv()
+            select_copy(h, t, q).wait_send()
+        send_ref[h, t] = (
+            jnp.dot(
+                weight_ref[h, t],
+                back_ref[h, t].reshape(slots, width),
+                preferred_element_type=f32,
+            )
+            .astype(bf16)
+            .reshape(2 * blocks, per, width)
+        )
+        pair_copy(h, t).start()
+
+        @pl.when((s != z) & outer)
+        def _():
+            for p in range(2):
+                onward(h, 1, p, s, m, sums(h, 1, p, t)).start()
+
+    def pair_sum(h, t, s, m):
+        pair_copy(h, t).wait_recv()
+        kept = sums(h, 0, 0, t)
+        kept[...] = (kept[...].astype(f32) + land_a[h, t].astype(f32)).astype(bf16)
+
+        @pl.when((s != z) & outer)
+        def _():
+            onward(h, 0, 0, s, m, kept).start()
+
+    def summed(h, k, p, slot, m):
+        if k == 0:
+            return sum_a.at[h, slot, m], ra_sem.at[h, slot, m]
+        return sum_b.at[h, p, slot, m], rb_sem.at[h, p, slot, m]
+
+    def landing(h, k, p, slot, m):
+        ref, recv = summed(h, k, p, slot, m)
+        remote(ref, ref, fs_sem.at[h, m], recv, near(h)).wait_recv()
+        return ref
+
+    def reduce(k, p, t, s, m):
+        for h in range(2):
+            ref = landing(h, k, p, s, m)
+            ref[...] = (
+                ref[...].astype(f32) + sums(h, k, p, t)[...].astype(f32)
+            ).astype(bf16)
+            onward(h, k, p, s, m, ref).start()
+
+    def gather(h, k, p, t, m):
+        first = jnp.where(z == depth - 1, depth, z)
+        total = sums(h, k, p, t)[...].astype(f32) + landing(h, k, p, first, m)[...].astype(f32)
+        ref, recv = summed(h, k, p, depth, m)
+
+        @pl.when(inner)
+        def _():
+            landing(h, k, p, depth, m)
+
+        return total + jnp.where(inner, ref[...].astype(f32), 0.0)
+
+    def final(t, m):
+        for h in range(2):
+            sums(h, 1, 1, t)[...] = gather(h, 1, 1, t, m).astype(bf16)
+            final_copy(h, m).start()
+
+    def finish(t, m):
+        span = pl.ds(m * rows_mb, rows_mb)
+        for h in range(2):
+            outs[h][span, 0:cut] = gather(h, 0, 0, t, m).astype(bf16).reshape(rows_mb, cut)
+            total = gather(h, 1, 0, t, m)
+            final_copy(h, m).wait_recv()
+            outs[h][span, cut:width] = (
+                (total + land_b[h, m].astype(f32)).astype(bf16).reshape(rows_mb, rest)
+            )
+
+    words = plan_words(depth, parts)
+    held = [
+        sum(jnp.where(z == k, words[k][b], 0) for k in range(depth))
+        for b in range(len(words[0]))
+    ]
+
+    def run(code):
+        kind = lax.div(code, count)
+        t = lax.rem(code, count)
+        s = lax.div(t, parts)
+        m = lax.rem(t, parts)
+
+        def on(low, high=None):
+            return pl.when(kind == low if high is None else (kind >= low) & (kind <= high))
+
+        @on(ARRIVE, ARRIVE + 2)
+        def _():
+            for n, (k, p) in enumerate(PIECES):
+                on(ARRIVE + n)(lambda k=k, p=p: arrive(k, p, s, m))
+
+        for h in range(2):
+            on(SELECT + h)(lambda h=h: select(h, t, s, m))
+        on(EXPERT)(lambda: expert(t))
+
+        @on(COMBINE, PAIR_SUM + 1)
+        def _():
+            for h in range(2):
+                on(COMBINE + h)(lambda h=h: combine(h, t, s, m))
+                on(PAIR_SUM + h)(lambda h=h: pair_sum(h, t, s, m))
+
+        @on(REDUCE, REDUCE + 2)
+        def _():
+            for n, (k, p) in enumerate(PIECES):
+                on(REDUCE + n)(lambda k=k, p=p: reduce(k, p, t, s, m))
+
+        @on(OWN, FINISH)
+        def _():
+            for n, (k, p) in enumerate(PIECES):
+                on(OWN + n)(lambda k=k, p=p: spread_own(k, p, m))
+            on(PASS_OWN)(lambda: pass_own(0, m))
+            on(FINAL)(lambda: final(t, m))
+            on(FINISH)(lambda: finish(t, m))
+
+    def block(b, carry):
+        word = sum(jnp.where(b == k, held[k], 0) for k in range(len(held)))
+
+        def one(n, word):
+            run(lax.rem(word, KINDS * count))
+            return lax.div(word, KINDS * count)
+
+        lax.fori_loop(0, PACKED, one, word)
+        return carry
+
+    lax.fori_loop(0, len(held), block, 0)
+
+    def drain(t, carry):
+        s = lax.div(t, parts)
+        m = lax.rem(t, parts)
+        for h in range(2):
+            spread_p(h, 0, s, m).wait_send()
+            pair_copy(h, t).wait_send()
+            for q in range(1, 4):
+                back_copy(h, t, q).wait_send()
+
+            @pl.when(s == z)
+            def _(h=h):
+                spread_p(h, 1, s, m).wait_send()
+                for k, p in PIECES:
+
+                    @pl.when(z < depth - 1)
+                    def _(k=k, p=p):
+                        spread_z(h, k, p, z, m, 1).wait_send()
+
+                    @pl.when(z > 0)
+                    def _(k=k, p=p):
+                        spread_z(h, k, p, z, m, -1, True).wait_send()
+
+            @pl.when(s != z)
+            def _(h=h):
+                for k, p in PIECES:
+                    onward(h, k, p, s, m, sums(h, k, p, t)).wait_send()
+
+                    @pl.when(inner)
+                    def _(k=k, p=p):
+                        spread_z(h, k, p, s, m, -away(s)).wait_send()
+
+        return carry
+
+    lax.fori_loop(0, count, drain, 0)
+    for m in range(parts):
+        for h in range(2):
+            final_copy(h, m).wait_send()
+
+
+def plane_cut(width):
+    blocks = width // LANES
+    return max(1, blocks * 5 // 9) * LANES
+
+
+def plane_local(
+    tokens, cotangent, expert_ids, combine_weights, live_counts, gate_weight, up_weight, down_weight
+):
+    groups = lax.axis_size("grp")
+    peers = lax.axis_size("dev")
+    experts = groups * peers
+    depth = groups // 2
+    rows, width = tokens.shape
+    hidden = gate_weight.shape[2]
+    parts = live_counts.shape[1]
+    rows_mb = rows // parts
+    per = rows_mb * expert_ids.shape[1] // experts
+    cut = plane_cut(width)
+    blocks = rows_mb // per
+    rest = width - cut
+    count = depth * parts
+    slots = 8 * per
+    vmem = pl.BlockSpec(memory_space=pltpu.VMEM)
+    anywhere = pl.BlockSpec(memory_space=pl.ANY)
+    dma = pltpu.SemaphoreType.DMA
+    bf16 = jnp.bfloat16
+    return pl.pallas_call(
+        functools.partial(plane_kernel, groups, parts, experts, per, cut),
+        out_shape=(
+            jax.ShapeDtypeStruct((rows, width), bf16),
+            jax.ShapeDtypeStruct((rows, width), bf16),
+        ),
+        in_specs=[anywhere] * 2 + [vmem] * 3 + [anywhere] * 3,
+        out_specs=(vmem, vmem),
+        scratch_shapes=[
+            pltpu.VMEM((width, hidden), bf16),
+            pltpu.VMEM((width, hidden), bf16),
+            pltpu.VMEM((hidden, width), bf16),
+            pltpu.VMEM((2, 2, depth, parts, rows_mb, cut + LANES), bf16),
+            pltpu.VMEM((2, 2, depth, parts, rows_mb, rest), bf16),
+            pltpu.VMEM((2, 2, LANES, slots), bf16),
+            pltpu.VMEM((2 * rows_mb, slots), jnp.float32),
+            pltpu.VMEM((2, count, 2 * rows_mb, slots), bf16),
+            pltpu.VMEM((2, count, 8, per, width), bf16),
+            pltpu.VMEM((count, 2, 2, 2, per, width), bf16),
+            pltpu.VMEM((count, 2, 2, 2, per, width), bf16),
+            pltpu.VMEM((2, count, 4, 2, per, width), bf16),
+            pltpu.VMEM((2, count, blocks, per, cut), bf16),
+            pltpu.VMEM((2, parts, blocks, per, rest), bf16),
+            pltpu.VMEM((2, depth + 1, parts, blocks, per, cut), bf16),
+            pltpu.VMEM((2, 2, depth + 1, parts, blocks, per, rest), bf16),
+            dma((3,)),
+            dma((4, parts)),
+            dma((4, 2, depth, parts)),
+            dma((4, 2, depth, parts)),
+            dma((4, 2, parts)),
+            dma((4, depth, parts)),
+            dma((2, count, 4)),
+            dma((2, count, 4)),
+            dma((2, count, 4)),
+            dma((2, count, 4)),
+            dma((2, count)),
+            dma((2, count)),
+            dma((2, depth + 1, parts)),
+            dma((2, 2, depth + 1, parts)),
+            dma((2, 3, depth, parts)),
+            dma((2, parts)),
+            dma((2, parts)),
+        ],
+        compiler_params=pltpu.CompilerParams(
+            collective_id=0, has_side_effects=True, vmem_limit_bytes=65 * 1024 * 1000
+        ),
+    )(
+        tokens,
+        cotangent,
+        expert_ids,
+        combine_weights,
+        live_counts,
+        gate_weight[0],
+        up_weight[0],
+        down_weight[0],
+    )
+
+
+def local(*args):
+    groups = lax.axis_size("grp")
+    peers = lax.axis_size("dev")
+    depth = groups // 2
+    fits = 2 * groups * peers <= LANES
+    planned = depth in PLANS and args[4].shape[1] == PLAN_PARTS
+    if peers == 4 and groups % 2 == 0 and planned and fits:
+        return plane_local(*args)
+    return general_local(*args)
+
+
 def solution(mesh):
     spec2 = P(("grp", "dev"), None)
     spec3 = P(("grp", "dev"), None, None)

time: 235 us -> 196 us (0.83); the launches traced: 235 us -> 193 us
  Pallas kernels: 224 us -> 186 us
  other arithmetic: 4.6 us -> 0 us
    pallas_call x1, Pallas kernels: 224 us -> 186 us  [plane_local(): pl.pallas_call(functools.partial(plane_kernel, groups, parts, experts, pe...]
    unnamed x2 -> x4, local copies, waits for them, and re-layouts: 3.83 us -> 6.65 us
where the time goes in v1:
time: 196 us; the launch traced here: 193 us
  Pallas kernels  186 us (95%)
  local copies, waits for them, and re-layouts  6.65 us (3%)
    pallas_call x1, Pallas kernels, plane_local(): pl.pallas_call(functools.partial(plane_kernel, groups, parts, experts, pe...  186 us
    unnamed x4, local copies, waits for them, and re-layouts  6.65 us

profile of v1, /device:TPU:0, one launch (start us, length us, event | category | flops | bytes accessed | tf_op | source)
XLA Modules:
  0.0 193.2 jit_solution(10862452354077310582)
XLA Ops:
  0.6 1.4 copy.11.mix_ref
  2.0 1.4 copy.10.ids_ref
  3.4 185.9 %shard_map.95 = (bf16[128,2304]{1,0:T(8,128)(2,1)}, bf16[128,2304]{1,0:T(8,128)(2,1)}) custom-call(bf16[128,2304]{1,0:T(8,128)(2,1)} %tok_hbm.1, bf16[128,2304]{1,0:T(8,128)(2,1)} %cot_hbm.1, s32[128,8]{1,0:T(8,128)} %copy.10.ids_ref, bf16[128,8]{1,0:T(8,128)(2,1)} %copy.11.mix_ref, s32[1,2]{1,0:T(1,128)} %live_ref.1, bf16[2304,512]{1,0:T(8,128)(2,1)} %bitcast.3, ...), custom_call_target="tpu_custom_call" | custom-call | tf_op jit(solution)/shard_map/pallas_call | solution.py:993
  189.3 1.9 copy.14
  191.3 1.9 copy.15

commit v2 on v1

--- a/solution.py
+++ b/solution.py
@@ -405,6 +405,7 @@
 
 
 LANES = 128
+SETTLE = 2
 
 
 PIECES = ((0, 0), (1, 0), (1, 1))
@@ -415,17 +416,17 @@
 PLAN_PARTS = 2
 PLAN_4 = (
     (
-        113, 129, 105, 120, 121, 2, 32, 24, 10, 18, 26, 34, 4, 40, 20, 42, 12, 28, 36, 50, 58,
-        6, 7, 44, 22, 14, 38, 30, 60, 15, 52, 23, 39, 31, 46, 68, 74, 3, 76, 47, 66, 62, 5, 54,
-        63, 19, 11, 55, 35, 27, 70, 71, 79, 21, 78, 13, 29, 37, 43, 45, 33, 51, 25, 61, 56, 53,
-        41, 77, 69, 48, 59, 136, 57, 49, 64, 67, 75, 137, 73, 72, 144, 65, 145,
+        129, 2, 120, 105, 24, 32, 10, 121, 18, 34, 26, 40, 4, 42, 113, 20, 12, 28, 36, 6, 58,
+        50, 44, 7, 74, 14, 66, 22, 52, 60, 30, 15, 38, 76, 68, 23, 31, 39, 46, 47, 3, 54, 19,
+        62, 55, 5, 63, 11, 27, 13, 70, 78, 35, 21, 29, 79, 71, 37, 43, 45, 33, 25, 59, 53, 48,
+        61, 41, 69, 77, 51, 56, 49, 75, 57, 137, 64, 67, 136, 72, 65, 73, 145, 144,
     ),
     (
-        122, 131, 34, 26, 4, 1, 20, 12, 0, 28, 36, 7, 16, 6, 8, 22, 24, 32, 9, 17, 44, 14, 15,
-        30, 38, 52, 33, 23, 31, 39, 107, 46, 25, 68, 5, 123, 40, 115, 60, 21, 47, 54, 13, 29,
-        62, 100, 76, 37, 48, 84, 41, 63, 94, 56, 78, 27, 102, 55, 95, 35, 45, 88, 103, 57, 71,
-        79, 70, 92, 49, 64, 42, 89, 96, 97, 86, 43, 72, 73, 87, 61, 53, 65, 58, 80, 93, 59, 50,
-        101, 138, 51, 81, 77, 69, 85, 139, 66, 74, 67, 75, 146, 147,
+        122, 26, 34, 4, 0, 20, 12, 28, 36, 8, 6, 16, 32, 1, 17, 24, 14, 44, 7, 9, 22, 30, 38,
+        40, 15, 23, 31, 39, 60, 115, 107, 56, 33, 123, 48, 47, 46, 63, 5, 55, 13, 25, 131, 54,
+        52, 100, 62, 21, 72, 92, 102, 41, 76, 94, 37, 35, 29, 95, 79, 78, 49, 70, 103, 27, 96,
+        86, 71, 45, 87, 68, 88, 42, 64, 53, 57, 80, 61, 84, 97, 89, 43, 93, 101, 58, 73, 50,
+        138, 65, 51, 81, 59, 77, 69, 85, 74, 139, 67, 66, 75, 146, 147,
     ),
 )
 PLANS = {4: PLAN_4}
@@ -659,30 +660,30 @@
     for load in loads:
         load.start()
 
-    row = lax.broadcasted_iota(jnp.int32, (rows, LANES), 0)
-    lane = lax.broadcasted_iota(jnp.int32, (rows, LANES), 1)
+    lane = lax.broadcasted_iota(jnp.int32, (LANES, rows), 0)
+    row = lax.broadcasted_iota(jnp.int32, (LANES, rows), 1)
     ids = ids_ref[...]
     mix = mix_ref[...].astype(f32)
-    weight = jnp.zeros((rows, LANES), f32)
-    named = jnp.zeros((rows, LANES), f32)
-    for k in range(ids.shape[1]):
-        expert_id = ids[:, k : k + 1]
-        weight = weight + jnp.where(lane == expert_id, mix[:, k : k + 1], 0.0)
+    weight = jnp.zeros((LANES, rows), f32)
+    named = jnp.zeros((LANES, rows), f32)
+    for k in range(ids.shape[0]):
+        expert_id = ids[k : k + 1]
+        weight = weight + jnp.where(lane == expert_id, mix[k : k + 1], 0.0)
         named = named + jnp.where(lane == expert_id + experts, 1.0, 0.0)
     lives = live_ref[...]
-    alive = jnp.zeros((rows, LANES), f32)
+    alive = jnp.zeros((LANES, rows), f32)
     for m in range(parts):
         first = m * rows_mb
         alive = alive + jnp.where(
             (row >= first) & (row < first + lives[0:1, m : m + 1]), 1.0, 0.0
         )
-    row_a = lax.broadcasted_iota(jnp.int32, (rows, rows), 0)
-    row_b = lax.broadcasted_iota(jnp.int32, (rows, rows), 1)
+    row_a = lax.broadcasted_iota(jnp.int32, (rows, rows), 1)
+    row_b = lax.broadcasted_iota(jnp.int32, (rows, rows), 0)
     before = jnp.where(
         (row_a > row_b) & (lax.div(row_a, rows_mb) == lax.div(row_b, rows_mb)), 1.0, 0.0
     ).astype(bf16)
-    rank = jnp.dot(before, named.astype(bf16), preferred_element_type=f32)
-    routes = jnp.where(lane < experts, weight * alive, rank).astype(bf16)
+    rank = jnp.dot(named.astype(bf16), before, preferred_element_type=f32)
+    routes = jnp.where(lane < experts, weight * alive, rank).T.astype(bf16)
     for h in range(2):
         for m in range(parts):
             dense_a[h, 0, z, m, :, cut : cut + LANES] = routes[m * rows_mb : (m + 1) * rows_mb]
@@ -964,6 +965,24 @@
             final_copy(h, m).wait_send()
 
 
+def settle_kernel(out_ref, grad_ref, out_to, grad_to):
+    out_to[...] = out_ref[...]
+    grad_to[...] = grad_ref[...]
+
+
+def settle(out, grad):
+    rows, width = out.shape
+    spec = pl.BlockSpec((rows // SETTLE, width), lambda i: (i, 0))
+    shape = jax.ShapeDtypeStruct(out.shape, out.dtype)
+    return pl.pallas_call(
+        settle_kernel,
+        grid=(SETTLE,),
+        out_shape=(shape, shape),
+        in_specs=[spec, spec],
+        out_specs=(spec, spec),
+    )(out, grad)
+
+
 def plane_cut(width):
     blocks = width // LANES
     return max(1, blocks * 5 // 9) * LANES
@@ -990,7 +1009,7 @@
     anywhere = pl.BlockSpec(memory_space=pl.ANY)
     dma = pltpu.SemaphoreType.DMA
     bf16 = jnp.bfloat16
-    return pl.pallas_call(
+    mixed = pl.pallas_call(
         functools.partial(plane_kernel, groups, parts, experts, per, cut),
         out_shape=(
             jax.ShapeDtypeStruct((rows, width), bf16),
@@ -1039,13 +1058,14 @@
     )(
         tokens,
         cotangent,
-        expert_ids,
-        combine_weights,
+        expert_ids.T,
+        combine_weights.T,
         live_counts,
         gate_weight[0],
         up_weight[0],
         down_weight[0],
     )
+    return settle(*mixed)
 
 
 def local(*args):

time: 196 us -> 189 us (0.964); the launches traced: 193 us -> 189 us
  local copies, waits for them, and re-layouts: 6.65 us -> 0 us
  Pallas kernels: 186 us -> 188 us
    unnamed x4 -> x0, local copies, waits for them, and re-layouts: 6.65 us -> none
    pallas_call x0 -> x1, Pallas kernels: none -> 2.11 us  [settle(): pl.pallas_call(settle_kernel, grid=(SETTLE,), out_shape=(shape, shape), i...]
where the time goes in v2:
time: 189 us
  Pallas kernels  188 us (99%)
    pallas_call x1, Pallas kernels, plane_local(): pl.pallas_call(functools.partial(plane_kernel, groups, parts, experts, pe...  186 us

profile of v2, /device:TPU:0, one launch (start us, length us, event | category | flops | bytes accessed | tf_op | source)
XLA Modules:
  0.0 188.8 jit_solution(10031654451140120383)
XLA Ops:
  0.6 186.0 %shard_map.95 = (bf16[128,2304]{1,0:T(8,128)(2,1)}, bf16[128,2304]{1,0:T(8,128)(2,1)}) custom-call(bf16[128,2304]{1,0:T(8,128)(2,1)} %tok_hbm.1, bf16[128,2304]{1,0:T(8,128)(2,1)} %cot_hbm.1, s32[8,128]{1,0:T(8,128)} %bitcast.8, bf16[8,128]{1,0:T(8,128)(2,1)} %bitcast.9, s32[1,2]{1,0:T(1,128)} %live_ref.1, bf16[2304,512]{1,0:T(8,128)(2,1)} %bitcast.5, ...), custom_call_target="tpu_custom_call" | custom-call | tf_op jit(solution)/shard_map/pallas_call | solution.py:1012
  186.7 2.1 %shard_map.96 = (bf16[128,2304]{1,0:T(8,128)(2,1)}, bf16[128,2304]{1,0:T(8,128)(2,1)}) custom-call(bf16[128,2304]{1,0:T(8,128)(2,1)} %get-tuple-element.4.out_ref, bf16[128,2304]{1,0:T(8,128)(2,1)} %get-tuple-element.5.grad_ref), custom_call_target="tpu_custom_call" | custom-call | tf_op jit(solution)/shard_map/pallas_call | solution.py:977

commit v3 on v2

--- a/solution.py
+++ b/solution.py
@@ -406,6 +406,8 @@
 
 LANES = 128
 SETTLE = 2
+SPREAD_SHARE = 10
+SUM_SHARE = 9
 
 
 PIECES = ((0, 0), (1, 0), (1, 1))
@@ -416,17 +418,17 @@
 PLAN_PARTS = 2
 PLAN_4 = (
     (
-        129, 2, 120, 105, 24, 32, 10, 121, 18, 34, 26, 40, 4, 42, 113, 20, 12, 28, 36, 6, 58,
-        50, 44, 7, 74, 14, 66, 22, 52, 60, 30, 15, 38, 76, 68, 23, 31, 39, 46, 47, 3, 54, 19,
-        62, 55, 5, 63, 11, 27, 13, 70, 78, 35, 21, 29, 79, 71, 37, 43, 45, 33, 25, 59, 53, 48,
-        61, 41, 69, 77, 51, 56, 49, 75, 57, 137, 64, 67, 136, 72, 65, 73, 145, 144,
+        120, 24, 32, 105, 2, 121, 129, 18, 10, 34, 113, 26, 4, 33, 25, 20, 42, 12, 36, 28, 6,
+        58, 50, 44, 22, 14, 66, 30, 38, 52, 7, 15, 60, 46, 74, 68, 76, 23, 39, 31, 11, 62, 13,
+        41, 47, 54, 5, 19, 63, 55, 21, 37, 29, 3, 79, 71, 45, 70, 35, 27, 49, 78, 61, 53, 43,
+        77, 40, 65, 69, 57, 51, 59, 48, 137, 67, 73, 75, 56, 136, 64, 72, 144, 145,
     ),
     (
-        122, 26, 34, 4, 0, 20, 12, 28, 36, 8, 6, 16, 32, 1, 17, 24, 14, 44, 7, 9, 22, 30, 38,
-        40, 15, 23, 31, 39, 60, 115, 107, 56, 33, 123, 48, 47, 46, 63, 5, 55, 13, 25, 131, 54,
-        52, 100, 62, 21, 72, 92, 102, 41, 76, 94, 37, 35, 29, 95, 79, 78, 49, 70, 103, 27, 96,
-        86, 71, 45, 87, 68, 88, 42, 64, 53, 57, 80, 61, 84, 97, 89, 43, 93, 101, 58, 73, 50,
-        138, 65, 51, 81, 59, 77, 69, 85, 74, 139, 67, 66, 75, 146, 147,
+        122, 34, 26, 4, 0, 16, 20, 12, 8, 28, 36, 1, 24, 32, 6, 22, 14, 9, 44, 7, 40, 15, 30,
+        17, 38, 52, 115, 60, 131, 48, 23, 39, 13, 107, 31, 123, 46, 25, 27, 33, 100, 92, 62,
+        76, 64, 5, 68, 84, 21, 47, 29, 35, 54, 42, 63, 56, 37, 102, 55, 41, 94, 95, 103, 96,
+        88, 45, 78, 70, 79, 43, 86, 71, 57, 87, 61, 49, 53, 89, 97, 101, 50, 65, 51, 58, 72,
+        80, 77, 93, 138, 69, 73, 85, 59, 66, 74, 81, 75, 139, 67, 146, 147,
     ),
 )
 PLANS = {4: PLAN_4}
@@ -443,6 +445,8 @@
                 kind - kind % count + (depth - 1 - kind % count // parts) * parts + kind % parts
                 for kind in codes
             ]
+        if codes.pop() != FINISH * count + (z + 1) * parts - 1:
+            raise ValueError("plan")
         orders.append(codes)
     length = max(len(codes) for codes in orders)
     length += -length % PACKED
@@ -464,6 +468,7 @@
     experts,
     per,
     cut,
+    back,
     tok_hbm,
     cot_hbm,
     ids_ref,
@@ -517,7 +522,6 @@
     rows_mb = dense_a.shape[4]
     rows = rows_mb * parts
     width = down_ref.shape[1]
-    rest = width - cut
     count = depth * parts
     pair = 2 * per
     blocks = rows_mb // per
@@ -528,7 +532,8 @@
     inner = (z > 0) & (z < depth - 1)
     outer = (z == 0) | (z == depth - 1)
     dense = (dense_a, dense_b)
-    size = (cut, rest)
+    size = (cut, width - cut)
+    sum_size = (back, width - back)
     outs = (out_ref, grad_ref)
 
     flips = (l + 2 - 4 * (l // 2), l + 1 - 2 * (l % 2))
@@ -552,17 +557,30 @@
             device_id_type=MESH,
         )
 
-    def spread_z(h, k, p, s, m, d, second=False):
-        slot = dense[k].at[h, p, s, m]
+    def block(h, k, p, s, m, tables):
+        extra = LANES if k == 0 and tables else 0
+        return dense[k].at[h, p, s, m, :, pl.ds(0, size[k] + extra)]
+
+    def by_part(k, m, fn):
+        if k == 1:
+            fn(False)
+        elif isinstance(m, int):
+            fn(m == 0)
+        else:
+            pl.when(m == 0)(lambda: fn(True))
+            pl.when(m != 0)(lambda: fn(False))
+
+    def spread_z(h, k, p, s, m, d, first, second=False):
+        slot = block(h, k, p, s, m, first and h == 0)
         send = agd_sem.at[2 * h + k, p, m] if second else agz_sem.at[2 * h + k, p, s, m]
         return remote(
             slot, slot, send, agr_sem.at[2 * h + k, p, s, m], {"grp": g + 2 * d, "dev": l}
         )
 
-    def spread_p(h, k, s, m):
+    def spread_p(h, k, s, m, first):
         return remote(
-            dense[k].at[h, 0, s, m],
-            dense[k].at[h, 1, s, m],
+            block(h, k, 0, s, m, first),
+            block(h, k, 1, s, m, first),
             agp_sem.at[2 * h + k, s, m],
             agr_sem.at[2 * h + k, 1, s, m],
             near(h),
@@ -592,8 +610,8 @@
         )
 
     def sums(h, k, p, t):
-        low = 0 if k == 0 else cut
-        return send_ref.at[h, t, pl.ds(p * blocks, blocks), :, pl.ds(low, size[k])]
+        low = 0 if k == 0 else back
+        return send_ref.at[h, t, pl.ds(p * blocks, blocks), :, pl.ds(low, sum_size[k])]
 
     def pair_copy(h, t):
         return remote(
@@ -650,7 +668,7 @@
                     in_sem.at[2 * h + k, m],
                 )
                 copy.start()
-                ins.append(copy)
+                ins.append((k, copy))
     loads = [
         pltpu.make_async_copy(src, dst, w_sem.at[n])
         for n, (src, dst) in enumerate(
@@ -660,14 +678,47 @@
     for load in loads:
         load.start()
 
+    def send_own(h, k, p, m, first):
+        @pl.when(z < depth - 1)
+        def _():
+            spread_z(h, k, p, z, m, 1, first).start()
+
+        @pl.when(z > 0)
+        def _():
+            spread_z(h, k, p, z, m, -1, first, True).start()
+
+    def spread_own(k, p, m):
+        def go(first):
+            for h in range(2):
+                if p == 1:
+                    spread_p(h, 1, z, m, first).wait_recv()
+                send_own(h, k, p, m, first)
+
+        by_part(k, m, go)
+
+    def pass_own(k, m):
+        def go(first):
+            for h in range(2):
+                spread_p(h, k, z, m, first).start()
+
+        by_part(k, m, go)
+
+    pl.semaphore_wait(barrier, 5 + jnp.where(inner, 2, 1))
+    for k, copy in ins:
+        if k == 1:
+            copy.wait()
+    pass_own(1, 0)
+    spread_own(1, 0, 0)
+
     lane = lax.broadcasted_iota(jnp.int32, (LANES, rows), 0)
     row = lax.broadcasted_iota(jnp.int32, (LANES, rows), 1)
+    shift = 2 * experts * lax.div(row, rows_mb)
     ids = ids_ref[...]
     mix = mix_ref[...].astype(f32)
     weight = jnp.zeros((LANES, rows), f32)
     named = jnp.zeros((LANES, rows), f32)
     for k in range(ids.shape[0]):
-        expert_id = ids[k : k + 1]
+        expert_id = ids[k : k + 1] + shift
         weight = weight + jnp.where(lane == expert_id, mix[k : k + 1], 0.0)
         named = named + jnp.where(lane == expert_id + experts, 1.0, 0.0)
     lives = live_ref[...]
@@ -683,10 +734,20 @@
         (row_a > row_b) & (lax.div(row_a, rows_mb) == lax.div(row_b, rows_mb)), 1.0, 0.0
     ).astype(bf16)
     rank = jnp.dot(named.astype(bf16), before, preferred_element_type=f32)
-    routes = jnp.where(lane < experts, weight * alive, rank).T.astype(bf16)
+    routes = (weight * alive + rank).T
+    packed = routes[0:rows_mb]
+    for m in range(1, parts):
+        packed = packed + routes[m * rows_mb : (m + 1) * rows_mb]
+    packed = packed.astype(bf16)
     for h in range(2):
-        for m in range(parts):
-            dense_a[h, 0, z, m, :, cut : cut + LANES] = routes[m * rows_mb : (m + 1) * rows_mb]
+        dense_a[h, 0, z, 0, :, cut : cut + LANES] = packed
+    for k, copy in ins:
+        if k == 0:
+            copy.wait()
+    spread_own(0, 0, 0)
+    pass_own(0, 0)
+    for m in range(1, parts):
+        pass_own(1, m)
 
     lane_k = lax.broadcasted_iota(jnp.int32, (LANES, slots), 0)
     slot_k = lax.broadcasted_iota(jnp.int32, (LANES, slots), 1)
@@ -694,62 +755,43 @@
     owner = 2 * z + core + lax.div(quad, 2) * (1 - 2 * core)
     for h in range(2):
         target = owner * peers + jnp.where(lax.rem(quad, 2) == 1, flips[h], l)
-        hot_ref[h, 0] = jnp.where(lane_k == target, 1.0, 0.0).astype(bf16)
-        hot_ref[h, 1] = jnp.where(lane_k == target + experts, 1.0, 0.0).astype(bf16)
+        for m in range(parts):
+            for n in range(2):
+                hot_ref[h, m, n] = jnp.where(
+                    lane_k == target + (2 * m + n) * experts, 1.0, 0.0
+                ).astype(bf16)
     row_s = lax.broadcasted_iota(jnp.int32, (both, slots), 0)
     col_s = lax.broadcasted_iota(jnp.int32, (both, slots), 1)
     slot_ref[...] = jnp.where(
         lax.div(row_s, rows_mb) == lax.rem(lax.div(col_s, per), 2), lax.rem(col_s, per), -1
     ).astype(f32)
 
-    for copy in ins:
-        copy.wait()
-    pl.semaphore_wait(barrier, 5 + jnp.where(inner, 2, 1))
-
-    def send_own(h, k, p, m):
-        @pl.when(z < depth - 1)
-        def _():
-            spread_z(h, k, p, z, m, 1).start()
-
-        @pl.when(z > 0)
-        def _():
-            spread_z(h, k, p, z, m, -1, True).start()
-
-    def spread_own(k, p, m):
-        for h in range(2):
-            if p == 1:
-                spread_p(h, 1, z, m).wait_recv()
-            send_own(h, k, p, m)
-
-    def pass_own(k, m):
-        for h in range(2):
-            spread_p(h, k, z, m).start()
-
-    pass_own(1, 0)
-    spread_own(0, 0, 0)
-    spread_own(1, 0, 0)
-    pass_own(0, 0)
-    for m in range(1, parts):
-        pass_own(1, m)
     for load in loads:
         load.wait()
 
     def arrive(k, p, s, m):
-        for h in range(2):
-            copy = spread_z(h, k, p, s, m, -away(s))
-            copy.wait_recv()
-            if k == 0:
-                spread_p(h, 0, s, m).start()
-
-            @pl.when(inner)
-            def _(copy=copy):
-                copy.start()
+        def go(first):
+            for h in range(2):
+                copy = spread_z(h, k, p, s, m, -away(s), first)
+                copy.wait_recv()
+                if k == 0:
+                    if h == 1 and first:
+                        dense_a[1, 0, s, 0, :, cut : cut + LANES] = dense_a[
+                            0, 0, s, 0, :, cut : cut + LANES
+                        ]
+                    spread_p(h, 0, s, m, first).start()
+
+                @pl.when(inner)
+                def _(copy=copy):
+                    copy.start()
+
+        by_part(k, m, go)
 
     def select(h, t, s, m):
-        spread_p(h, 0, s, m).wait_recv()
-        routes = dense_a[h, :, s, m, :, cut : cut + LANES].reshape(both, LANES)
-        weights = jnp.dot(routes, hot_ref[h, 0], preferred_element_type=f32)
-        ranks = jnp.dot(routes, hot_ref[h, 1], preferred_element_type=f32)
+        by_part(0, m, lambda first: spread_p(h, 0, s, m, first).wait_recv())
+        routes = dense_a[h, :, s, 0, :, cut : cut + LANES].reshape(both, LANES)
+        weights = jnp.dot(routes, hot_ref[h, m, 0], preferred_element_type=f32)
+        ranks = jnp.dot(routes, hot_ref[h, m, 1], preferred_element_type=f32)
         weights = jnp.where(ranks == slot_ref[...], weights, 0.0)
         weight_ref[h, t] = weights.astype(bf16)
         pick = jnp.where(weights != 0.0, 1.0, 0.0).T.astype(bf16)
@@ -864,11 +906,11 @@
     def finish(t, m):
         span = pl.ds(m * rows_mb, rows_mb)
         for h in range(2):
-            outs[h][span, 0:cut] = gather(h, 0, 0, t, m).astype(bf16).reshape(rows_mb, cut)
+            outs[h][span, 0:back] = gather(h, 0, 0, t, m).astype(bf16).reshape(rows_mb, back)
             total = gather(h, 1, 0, t, m)
             final_copy(h, m).wait_recv()
-            outs[h][span, cut:width] = (
-                (total + land_b[h, m].astype(f32)).astype(bf16).reshape(rows_mb, rest)
+            outs[h][span, back:width] = (
+                (total + land_b[h, m].astype(f32)).astype(bf16).reshape(rows_mb, width - back)
             )
 
     words = plan_words(depth, parts)
@@ -914,7 +956,7 @@
             on(FINAL)(lambda: final(t, m))
             on(FINISH)(lambda: finish(t, m))
 
-    def block(b, carry):
+    def batch(b, carry):
         word = sum(jnp.where(b == k, held[k], 0) for k in range(len(held)))
 
         def one(n, word):
@@ -924,38 +966,43 @@
         lax.fori_loop(0, PACKED, one, word)
         return carry
 
-    lax.fori_loop(0, len(held), block, 0)
+    lax.fori_loop(0, len(held), batch, 0)
 
     def drain(t, carry):
         s = lax.div(t, parts)
         m = lax.rem(t, parts)
         for h in range(2):
-            spread_p(h, 0, s, m).wait_send()
             pair_copy(h, t).wait_send()
             for q in range(1, 4):
                 back_copy(h, t, q).wait_send()
-
-            @pl.when(s == z)
-            def _(h=h):
-                spread_p(h, 1, s, m).wait_send()
-                for k, p in PIECES:
-
-                    @pl.when(z < depth - 1)
-                    def _(k=k, p=p):
-                        spread_z(h, k, p, z, m, 1).wait_send()
-
-                    @pl.when(z > 0)
-                    def _(k=k, p=p):
-                        spread_z(h, k, p, z, m, -1, True).wait_send()
+        for k, p in PIECES:
+
+            def go(first, k=k, p=p):
+                for h in range(2):
+                    if p == 0:
+
+                        @pl.when((s == z) | (k == 0))
+                        def _(h=h):
+                            spread_p(h, k, s, m, first).wait_send()
+
+                    @pl.when((s == z) & (z < depth - 1))
+                    def _(h=h):
+                        spread_z(h, k, p, z, m, 1, first).wait_send()
+
+                    @pl.when((s == z) & (z > 0))
+                    def _(h=h):
+                        spread_z(h, k, p, z, m, -1, first, True).wait_send()
+
+                    @pl.when((s != z) & inner)
+                    def _(h=h):
+                        spread_z(h, k, p, s, m, -away(s), first).wait_send()
+
+            by_part(k, m, go)
 
             @pl.when(s != z)
-            def _(h=h):
-                for k, p in PIECES:
+            def _(k=k, p=p):
+                for h in range(2):
                     onward(h, k, p, s, m, sums(h, k, p, t)).wait_send()
-
-                    @pl.when(inner)
-                    def _(k=k, p=p):
-                        spread_z(h, k, p, s, m, -away(s)).wait_send()
 
         return carry
 
@@ -963,6 +1010,7 @@
     for m in range(parts):
         for h in range(2):
             final_copy(h, m).wait_send()
+    finish(z * parts + parts - 1, parts - 1)
 
 
 def settle_kernel(out_ref, grad_ref, out_to, grad_to):
@@ -983,9 +1031,9 @@
     )(out, grad)
 
 
-def plane_cut(width):
+def plane_cut(width, share):
     blocks = width // LANES
-    return max(1, blocks * 5 // 9) * LANES
+    return max(1, blocks * share // 18) * LANES
 
 
 def plane_local(
@@ -1000,7 +1048,8 @@
     parts = live_counts.shape[1]
     rows_mb = rows // parts
     per = rows_mb * expert_ids.shape[1] // experts
-    cut = plane_cut(width)
+    cut = plane_cut(width, SPREAD_SHARE)
+    back = plane_cut(width, SUM_SHARE)
     blocks = rows_mb // per
     rest = width - cut
     count = depth * parts
@@ -1010,7 +1059,7 @@
     dma = pltpu.SemaphoreType.DMA
     bf16 = jnp.bfloat16
     mixed = pl.pallas_call(
-        functools.partial(plane_kernel, groups, parts, experts, per, cut),
+        functools.partial(plane_kernel, groups, parts, experts, per, cut, back),
         out_shape=(
             jax.ShapeDtypeStruct((rows, width), bf16),
             jax.ShapeDtypeStruct((rows, width), bf16),
@@ -1023,17 +1072,17 @@
             pltpu.VMEM((hidden, width), bf16),
             pltpu.VMEM((2, 2, depth, parts, rows_mb, cut + LANES), bf16),
             pltpu.VMEM((2, 2, depth, parts, rows_mb, rest), bf16),
-            pltpu.VMEM((2, 2, LANES, slots), bf16),
+            pltpu.VMEM((2, parts, 2, LANES, slots), bf16),
             pltpu.VMEM((2 * rows_mb, slots), jnp.float32),
             pltpu.VMEM((2, count, 2 * rows_mb, slots), bf16),
             pltpu.VMEM((2, count, 8, per, width), bf16),
             pltpu.VMEM((count, 2, 2, 2, per, width), bf16),
             pltpu.VMEM((count, 2, 2, 2, per, width), bf16),
             pltpu.VMEM((2, count, 4, 2, per, width), bf16),
-            pltpu.VMEM((2, count, blocks, per, cut), bf16),
-            pltpu.VMEM((2, parts, blocks, per, rest), bf16),
-            pltpu.VMEM((2, depth + 1, parts, blocks, per, cut), bf16),
-            pltpu.VMEM((2, 2, depth + 1, parts, blocks, per, rest), bf16),
+            pltpu.VMEM((2, count, blocks, per, back), bf16),
+            pltpu.VMEM((2, parts, blocks, per, width - back), bf16),
+            pltpu.VMEM((2, depth + 1, parts, blocks, per, back), bf16),
+            pltpu.VMEM((2, 2, depth + 1, parts, blocks, per, width - back), bf16),
             dma((3,)),
             dma((4, parts)),
             dma((4, 2, depth, parts)),
@@ -1072,7 +1121,7 @@
     groups = lax.axis_size("grp")
     peers = lax.axis_size("dev")
     depth = groups // 2
-    fits = 2 * groups * peers <= LANES
+    fits = 2 * PLAN_PARTS * groups * peers <= LANES
     planned = depth in PLANS and args[4].shape[1] == PLAN_PARTS
     if peers == 4 and groups % 2 == 0 and planned and fits:
         return plane_local(*args)

time: 189 us -> 188 us (level)
  no operation moved by 1% of the time
where the time goes in v3:
time: 188 us
  Pallas kernels  187 us (99%)
    pallas_call x1, Pallas kernels, plane_local(): pl.pallas_call(functools.partial(plane_kernel, groups, parts, experts, pe...  185 us

profile of v3, /device:TPU:0, one launch (start us, length us, event | category | flops | bytes accessed | tf_op | source)
XLA Modules:
  0.0 188.0 jit_solution(14903067060157305430)
XLA Ops:
  0.6 185.3 %shard_map.95 = (bf16[128,2304]{1,0:T(8,128)(2,1)}, bf16[128,2304]{1,0:T(8,128)(2,1)}) custom-call(bf16[128,2304]{1,0:T(8,128)(2,1)} %tok_hbm.1, bf16[128,2304]{1,0:T(8,128)(2,1)} %cot_hbm.1, s32[8,128]{1,0:T(8,128)} %bitcast.8, bf16[8,128]{1,0:T(8,128)(2,1)} %bitcast.9, s32[1,2]{1,0:T(1,128)} %live_ref.1, bf16[2304,512]{1,0:T(8,128)(2,1)} %bitcast.5, ...), custom_call_target="tpu_custom_call" | custom-call | tf_op jit(solution)/shard_map/pallas_call | solution.py:1061
  185.9 2.1 %shard_map.96 = (bf16[128,2304]{1,0:T(8,128)(2,1)}, bf16[128,2304]{1,0:T(8,128)(2,1)}) custom-call(bf16[128,2304]{1,0:T(8,128)(2,1)} %get-tuple-element.4.out_ref, bf16[128,2304]{1,0:T(8,128)(2,1)} %get-tuple-element.5.grad_ref), custom_call_target="tpu_custom_call" | custom-call | tf_op jit(solution)/shard_map/pallas_call | solution.py:1025
